TPU v7x, 256 devices: a whole 4x4x8 slice. The times are simulated.
256 devices in a mesh: ctx: 16 (over y_hi, z), head: 16 (over y_lo, x, core).
Axes of the slice: x: 4, y: 4 (y_hi: 2, y_lo: 2; y = y_hi * 2 + y_lo), z: 8, core: 2. Of those that a mesh axis runs over, the one named last changes fastest.
Arguments:
- q_nope: bfloat16 [4096, 16384], P('ctx', 'head'), may hold values from -4 to 4
- q_rope: bfloat16 [4096, 8192], P('ctx', 'head'), may hold values from -8 to 8
- kv_latent: bfloat16 [4096, 576], P(('ctx', 'head')), may hold values from -6 to 6
- half_order: int32 [32], replicated, may hold values from 0 to 31, as said below
- w_uk: bfloat16 [128, 128, 512], P('head'), may hold values from -0.5 to 0.5
- w_uv: bfloat16 [128, 512, 128], P('head'), may hold values from -1.5 to 1.5
Outputs:
- attended: bfloat16 [4096, 16384], P('ctx', 'head')
Inputs may be any that keep to these rules, and one draw needn't show every extreme that they name: `half_order`: a permutation of 0 to 31.
All inputs are finite; a program needn't handle non-finite values.
Results may differ from a plain program's by a relative error of at most 0.0085.
Values may be sent and summed in bfloat16 or wider, within the bound.
No kernel may reach another device: no remote copies, remote signals or barrier semaphores. Data moves between devices by JAX's collectives and lax.ppermute only.
A program may use at most 64 MiB of HBM per device.

v0:
```python
import functools

import jax
import jax.numpy as jnp
import numpy as np
from jax import lax
from jax.experimental import pallas as pl
from jax.experimental.pallas import tpu as pltpu
from jax.sharding import Mesh
from jax.sharding import PartitionSpec as P


HEADS = 8
ROWS = 256
NOPE = 128
LATENT = 512
ROPE = 64
PIECE = 512
SCALE = (NOPE + ROPE) ** -0.5 * 1.4426950408889634
LOW = -1e30
NT = (((1,), (1,)), ((), ()))
NN = (((1,), (0,)), ((), ()))
HEAD_TILE = 2
TILES = HEADS // HEAD_TILE
NY = 4
CALLS = ((0, 1), (2,), (3, 4), (5, 6), (7,))


def ring_step(value):
    pairs = [
        (y * 2 + c, ((y + (1 - 2 * c)) % NY) * 2 + c) for y in range(NY) for c in range(2)
    ]
    return lax.ppermute(value, ("yh", "yl", "c"), pairs)


def exchange(value):
    return lax.ppermute(value, "c", [(0, 1), (1, 0)])


def key_positions(half_order):
    y = lax.axis_index("yh") * 2 + lax.axis_index("yl")
    c = lax.axis_index("c")
    ahead = 1 - 2 * c
    ys = jnp.stack([y, y, y - ahead, y + ahead, y - ahead, y + ahead, y + 2, y + 2]) & 3
    cs = jnp.stack([c, 1 - c, c, 1 - c, 1 - c, c, c, 1 - c])
    table = half_order.reshape(2, 8, 2).transpose(0, 2, 1).reshape(4, 8)
    block = jnp.sum(
        jnp.where((ys[:, None] == jnp.arange(4)[None, :])[:, :, None], table[None], 0), axis=1
    )
    j = np.arange(64)
    inner = jnp.asarray((j // 16) * 32 + j % 16, jnp.int32)
    pos = block[:, :, None] * 128 + inner[None, None, :] + cs[:, None, None] * 16
    return pos.reshape(8, PIECE).astype(jnp.int32)


def query_positions(half_order):
    ctx = lax.axis_index("yh") * 8 + lax.axis_index("z")
    block = lax.dynamic_slice(half_order, (ctx * 2,), (2,))
    pos = (block[:, None] * 128 + jnp.arange(128, dtype=jnp.int32)[None, :]).reshape(ROWS, 1)
    return jnp.broadcast_to(pos, (ROWS, 128))


def pack_queries(qn, qr, qx):
    zeros = jnp.zeros((ROWS, 64), jnp.bfloat16)
    for h in range(HEADS):
        rows = slice(h * ROWS, (h + 1) * ROWS)
        qx[rows, 0:128] = qn[:, h * 128 : (h + 1) * 128]
        qx[rows, 128:256] = jnp.concatenate([qr[:, h * 64 : (h + 1) * 64], zeros], axis=1)


def attend(first, last, ids, *refs):
    f32, bf16 = jnp.float32, jnp.bfloat16
    refs = list(refs)
    take = lambda n: [refs.pop(0) for _ in range(n)]
    qpos, kpos, qx, wuk = take(4)
    pieces = take(len(ids))
    wuv = take(1)[0] if last else None
    state = None if first else take(3)
    if last:
        out = take(1)[0]
        acc, mref, lref = state
    else:
        acc, mref, lref = take(3)
    kv, kp, kn, kr, sbuf = take(5)
    zk = jnp.zeros((PIECE, 64), bf16)
    blocks = len(ids)

    def expand(a, b):
        def go(slot):
            kn[:, a * 128 : b * 128] = lax.dot_general(
                kv[slot], wuk[a * 128 : b * 128, :], NT, preferred_element_type=f32
            ).astype(bf16)

        return go

    def score(kb, tile, slot, i):
        h = tile * HEAD_TILE + i
        keys = jnp.concatenate([kn[:, h * 128 : (h + 1) * 128], kr[kb]], axis=1)
        sbuf[slot, i * ROWS : (i + 1) * ROWS, :] = lax.dot_general(
            qx[h * ROWS : (h + 1) * ROWS, :], keys, NT, preferred_element_type=f32
        )

    def weigh(kb, tile, slot, i, fresh):
        r0 = (tile * HEAD_TILE + i) * ROWS
        r1 = r0 + ROWS
        a, b = i * ROWS, (i + 1) * ROWS
        qp = qpos[...]
        s = [
            jnp.where(
                kp[kb, 0:1, c * 128 : (c + 1) * 128] <= qp,
                sbuf[slot, a:b, c * 128 : (c + 1) * 128],
                LOW,
            )
            for c in range(PIECE // 128)
        ]
        top = functools.reduce(jnp.maximum, s)
        top = jnp.max(top, axis=1, keepdims=True)
        if fresh:
            new = jnp.broadcast_to(top, (ROWS, 128))
        else:
            old = mref[r0:r1, :]
            new = jnp.maximum(old, top)
            factor = jnp.exp2((old - new) * SCALE)
        base = new * SCALE
        w = [jnp.exp2(v * SCALE - base) for v in s]
        total = functools.reduce(jnp.add, w)
        mref[r0:r1, :] = new
        lref[r0:r1, :] = total if fresh else lref[r0:r1, :] * factor + total
        wb = jnp.concatenate([v.astype(bf16) for v in w], axis=1)
        product = lax.dot_general(wb, kv[kb], NN, preferred_element_type=f32)
        if fresh:
            acc[r0:r1, :] = product
        else:
            for c in range(LATENT // 128):
                cols = slice(c * 128, (c + 1) * 128)
                acc[r0:r1, cols] = acc[r0:r1, cols] * factor + product[:, cols]

    for n, piece in enumerate(ids):
        rows = pieces[n][...].reshape(PIECE, LATENT + ROPE)
        kv[n] = rows[:, 0:LATENT]
        kr[n] = jnp.concatenate([rows[:, LATENT:], zk], axis=1)
        kp[n, 0:1, :] = kpos[piece : piece + 1, :]

    def block(kb, fresh):
        for t in range(TILES):
            expand(t * HEAD_TILE, (t + 1) * HEAD_TILE)(kb)
            if t == 0:
                for i in range(HEAD_TILE):
                    score(kb, 0, 0, i)
                continue
            for i in range(HEAD_TILE):
                score(kb, t, t % 2, i)
                weigh(kb, t - 1, (t - 1) % 2, i, fresh)
        for i in range(HEAD_TILE):
            weigh(kb, TILES - 1, (TILES - 1) % 2, i, fresh)

    if blocks == 1:
        block(0, first)
    else:
        if first:
            mref[...] = jnp.full_like(mref, LOW)
            lref[...] = jnp.zeros_like(lref)
            acc[...] = jnp.zeros_like(acc)

        def body(kb, carry):
            block(kb, False)
            return carry

        lax.fori_loop(0, blocks, body, 0)
    if last:
        for h in range(HEADS):
            r0 = h * ROWS
            den = jnp.sum(lref[r0 : r0 + ROWS, :], axis=1, keepdims=True)
            latent = (acc[r0 : r0 + ROWS, :] / den).astype(bf16)
            out[:, h * 128 : (h + 1) * 128] = jnp.dot(
                latent, wuv[h], preferred_element_type=f32
            ).astype(bf16)


def attend_call(first, last, ids, qpos, kpos, qx, wuk, pieces, wuv, state):
    vmem = pltpu.VMEM
    f32, bf16 = jnp.float32, jnp.bfloat16
    args = [qpos, kpos, qx, wuk, *pieces]
    if last:
        args.append(wuv)
    alias = {}
    if not first:
        if not last:
            alias = {len(args) + i: i for i in range(3)}
        args.extend(state)
    shapes = [
        jax.ShapeDtypeStruct((HEADS * ROWS, LATENT), f32),
        jax.ShapeDtypeStruct((HEADS * ROWS, 128), f32),
        jax.ShapeDtypeStruct((HEADS * ROWS, 128), f32),
    ]
    n = len(ids)
    scratch = [
        vmem((n, PIECE, LATENT), bf16),
        vmem((n, 8, PIECE), jnp.int32),
        vmem((PIECE, HEADS * 128), bf16),
        vmem((n, PIECE, 128), bf16),
        vmem((2, HEAD_TILE * ROWS, PIECE), f32),
    ]
    out_shape = jax.ShapeDtypeStruct((ROWS, HEADS * 128), bf16) if last else shapes
    spec = pl.BlockSpec(memory_space=vmem)
    keys = n * PIECE
    return pl.pallas_call(
        functools.partial(attend, first, last, ids),
        out_shape=out_shape,
        in_specs=[spec] * len(args),
        out_specs=spec if last else [spec] * 3,
        scratch_shapes=scratch,
        input_output_aliases=alias,
        compiler_params=pltpu.CompilerParams(vmem_limit_bytes=14 << 20),
        cost_estimate=pl.CostEstimate(
            flops=2 * HEADS * ROWS * keys * 1024,
            bytes_accessed=1 << 20,
            transcendentals=HEADS * ROWS * keys,
        ),
    )(*args)


def compute(q_nope, q_rope, kv_latent, half_order, w_uk, w_uv):
    bf16 = jnp.bfloat16
    wuk = w_uk.reshape(HEADS * NOPE, LATENT)
    copies = jnp.broadcast_to(kv_latent[None], (32, *kv_latent.shape))
    plane = lax.all_to_all(copies, ("z", "x"), 0, 0, tiled=True)
    qpos = query_positions(half_order)
    kpos = key_positions(half_order)
    spec = pl.BlockSpec(memory_space=pltpu.VMEM)
    qx = pl.pallas_call(
        pack_queries,
        out_shape=jax.ShapeDtypeStruct((HEADS * ROWS, 256), bf16),
        in_specs=[spec] * 2,
        out_specs=spec,
        compiler_params=pltpu.CompilerParams(vmem_limit_bytes=8 << 20),
        name="pack_queries",
    )(q_nope, q_rope)
    first = ring_step(plane)
    other = exchange(plane)
    second = ring_step(other)
    third = ring_step(first)
    first_other = exchange(first)
    second_other = exchange(second)
    third_other = exchange(third)
    pieces = (plane, other, first, first_other, second, second_other, third, third_other)
    state = None
    for n, ids in enumerate(CALLS):
        state = attend_call(
            n == 0,
            n == len(CALLS) - 1,
            ids,
            qpos,
            kpos,
            qx,
            wuk,
            [pieces[i] for i in ids],
            w_uv,
            state,
        )
    return state


def solution(mesh):
    split = Mesh(mesh.devices.reshape(2, 8, 2, 4, 2), ("yh", "z", "yl", "x", "c"))
    ctx, head = ("yh", "z"), ("yl", "x", "c")
    return jax.shard_map(
        compute,
        mesh=split,
        in_specs=(
            P(ctx, head),
            P(ctx, head),
            P((*ctx, *head), None),
            P(),
            P(head, None, None),
            P(head, None, None),
        ),
        out_specs=P(ctx, head),
        check_vma=False,
    )
```

profile of v0, /device:TPU:1, one launch (start us, length us, event | category | flops | bytes accessed | tf_op | source)
XLA Modules:
  0.0 79.1 jit_solution(14448537824365744691)
XLA Ops:
  0.0 1.7 %broadcast_in_dim.46 = bf16[32,16,576]{2,1,0:T(8,128)(2,1)} broadcast(bf16[16,576]{1,0:T(8,128)(2,1)} %param.9), dimensions={1,2} | broadcast | bytes 608256 | tf_op jit(solution)/shard_map/broadcast_in_dim | solution.py:226
  1.7 11.9 %all-to-all-start = ((bf16[32,16,576]{2,1,0:T(8,128)(2,1)}), bf16[32,16,576]{2,1,0:T(8,128)(2,1)S(1)}, u32[]{:S(2)}, u32[]{:S(2)}) async-start(bf16[32,16,576]{2,1,0:T(8,128)(2,1)} %broadcast_in_dim.46), calls=%async_computation | async-start | bytes 1310720 | tf_op jit(solution)/shard_map/all_to_all | solution.py:227
  13.6 0.7 reshape.184
  14.3 0.1 copy.19
  14.6 17.7 %all-to-all-done.refs_4_ = bf16[32,16,576]{2,1,0:T(8,128)(2,1)S(1)} async-done(((bf16[32,16,576]{2,1,0:T(8,128)(2,1)}), bf16[32,16,576]{2,1,0:T(8,128)(2,1)S(1)}, u32[]{:S(2)}, u32[]{:S(2)}) %all-to-all-start) | async-done | bytes 589856 | tf_op jit(solution)/shard_map/all_to_all | solution.py:227
  32.3 2.5 %collective-permute-start.3 = (bf16[32,16,576]{2,1,0:T(8,128)(2,1)S(1)}, bf16[32,16,576]{2,1,0:T(8,128)(2,1)S(1)}, u32[]{:S(2)}, u32[]{:S(2)}) collective-permute-start(bf16[32,16,576]{2,1,0:T(8,128)(2,1)S(1)} %all-to-all-done.refs_4_), channel_id=1, source_target_pairs={{0,1},{1,0},{2,3},{3,2},{4,5},{5,4},{6,7},{7,6},{8,9},{9,8},{10,11... | collective-permute-start | bytes 1769480 | tf_op jit(solution)/shard_map/ppermute | solution.py:37
  34.8 2.7 %collective-permute-start = (bf16[32,16,576]{2,1,0:T(8,128)(2,1)S(1)}, bf16[32,16,576]{2,1,0:T(8,128)(2,1)S(1)}, u32[]{:S(2)}, u32[]{:S(2)}) collective-permute-start(bf16[32,16,576]{2,1,0:T(8,128)(2,1)S(1)} %all-to-all-done.refs_4_), channel_id=1, source_target_pairs={{0,8},{1,137},{8,128},{9,1},{128,136},{129,9},{136,0},{137,129},{2... | collective-permute-start | bytes 1769480 | tf_op jit(solution)/shard_map/ppermute | solution.py:33
  37.7 0.7 add.77
  38.5 1.0 %copy-done.2 = bf16[256,1024]{1,0:T(8,128)(2,1)S(1)} copy-done((bf16[256,1024]{1,0:T(8,128)(2,1)S(1)}, bf16[256,1024]{1,0:T(8,128)(2,1)}, u32[]{:S(2)}) %copy-start.2) | copy-done | bytes 524312
  39.5 0.9 %copy-done.3 = bf16[256,512]{1,0:T(8,128)(2,1)S(1)} copy-done((bf16[256,512]{1,0:T(8,128)(2,1)S(1)}, bf16[256,512]{1,0:T(8,128)(2,1)}, u32[]{:S(2)}) %copy-start.3) | copy-done | bytes 262168
  40.5 0.2 pack_queries.1.refs_2_
  40.7 0.7 dynamic-slice_multiply_fusion
  41.5 0.5 collective-permute-start.4
  42.0 3.1 %collective-permute-done.refs_4_ = bf16[32,16,576]{2,1,0:T(8,128)(2,1)S(1)} collective-permute-done((bf16[32,16,576]{2,1,0:T(8,128)(2,1)S(1)}, bf16[32,16,576]{2,1,0:T(8,128)(2,1)S(1)}, u32[]{:S(2)}, u32[]{:S(2)}) %collective-permute-start) | collective-permute-done | bytes 589856 | tf_op jit(solution)/shard_map/ppermute | solution.py:33
  45.1 1.5 %collective-permute-start.6 = (bf16[32,16,576]{2,1,0:T(8,128)(2,1)S(1)}, bf16[32,16,576]{2,1,0:T(8,128)(2,1)S(1)}, u32[]{:S(2)}, u32[]{:S(2)}) collective-permute-start(bf16[32,16,576]{2,1,0:T(8,128)(2,1)S(1)} %collective-permute-done.refs_4_), channel_id=1, source_target_pairs={{0,1},{1,0},{2,3},{3,2},{4,5},{5,4},{6,7},{7,6},{8,9},{9,8},{10,11... | collective-permute-start | bytes 1769480 | tf_op jit(solution)/shard_map/ppermute | solution.py:37
  46.7 1.6 %collective-permute-start.1 = (bf16[32,16,576]{2,1,0:T(8,128)(2,1)S(1)}, bf16[32,16,576]{2,1,0:T(8,128)(2,1)S(1)}, u32[]{:S(2)}, u32[]{:S(2)}) collective-permute-start(bf16[32,16,576]{2,1,0:T(8,128)(2,1)S(1)} %collective-permute-done.refs_4_), channel_id=1, source_target_pairs={{0,8},{1,137},{8,128},{9,1},{128,136},{129,9},{136,0},{137,129},{2... | collective-permute-start | bytes 1769480 | tf_op jit(solution)/shard_map/ppermute | solution.py:33
  48.3 7.2 %shard_map.73 = (f32[2048,512]{1,0:T(8,128)S(1)}, f32[2048,128]{1,0:T(8,128)S(1)}, f32[2048,128]{1,0:T(8,128)S(1)}) custom-call(s32[256,128]{1,0:T(8,128)S(1)} %broadcast_in_dim.26.refs_0_, s32[8,512]{1,0:T(8,128)S(1)} %add_add_fusion.refs_1_, bf16[2048,256]{1,0:T(8,128)(2,1)S(1)} %pack_queries.1.refs_2_, bf16[1024,512]{1,0:T(8,128)(2,1)S(1)} %bitcast.11, ...), custom_call_target="tpu_custom_call" | custom-call | flops 4294967296 | bytes 1048576 | tf_op jit(solution)/shard_map/pallas_call | solution.py:207
  55.6 0.1 collective-permute-start.5
  55.7 3.3 %shard_map.74 = (f32[2048,512]{1,0:T(8,128)S(1)}, f32[2048,128]{1,0:T(8,128)S(1)}, f32[2048,128]{1,0:T(8,128)S(1)}) custom-call(s32[256,128]{1,0:T(8,128)S(1)} %broadcast_in_dim.26.refs_0_, s32[8,512]{1,0:T(8,128)S(1)} %add_add_fusion.refs_1_, bf16[2048,256]{1,0:T(8,128)(2,1)S(1)} %pack_queries.1.refs_2_, ...), custom_call_target="tpu_custom_call", output_to_operand_aliasing={{0}: (5, {}), {1}: (6, {}), {2}: (7, {})} | custom-call | flops 2147483648 | bytes 1048576 | tf_op jit(solution)/shard_map/pallas_call | solution.py:207
  59.0 0.2 collective-permute-done.1.refs_5_
  59.2 1.5 %collective-permute-start.2 = (bf16[32,16,576]{2,1,0:T(8,128)(2,1)S(1)}, bf16[32,16,576]{2,1,0:T(8,128)(2,1)S(1)}, u32[]{:S(2)}, u32[]{:S(2)}) collective-permute-start(bf16[32,16,576]{2,1,0:T(8,128)(2,1)S(1)} %collective-permute-done.1.refs_5_), channel_id=1, source_target_pairs={{0,1},{1,0},{2,3},{3,2},{4,5},{5,4},{6,7},{7,6},{8,9},{9,8},{10,11... | collective-permute-start | bytes 1769480 | tf_op jit(solution)/shard_map/ppermute | solution.py:37
  60.7 6.8 %shard_map.75 = (f32[2048,512]{1,0:T(8,128)S(1)}, f32[2048,128]{1,0:T(8,128)S(1)}, f32[2048,128]{1,0:T(8,128)S(1)}) custom-call(s32[256,128]{1,0:T(8,128)S(1)} %broadcast_in_dim.26.refs_0_, s32[8,512]{1,0:T(8,128)S(1)} %add_add_fusion.refs_1_, bf16[2048,256]{1,0:T(8,128)(2,1)S(1)} %pack_queries.1.refs_2_, ...), custom_call_target="tpu_custom_call", output_to_operand_aliasing={{0}: (6, {}), {1}: (7, {}), {2}: (8, {})} | custom-call | flops 4294967296 | bytes 1048576 | tf_op jit(solution)/shard_map/pallas_call | solution.py:207
  67.5 6.8 %shard_map.76 = (f32[2048,512]{1,0:T(8,128)S(1)}, f32[2048,128]{1,0:T(8,128)S(1)}, f32[2048,128]{1,0:T(8,128)S(1)}) custom-call(s32[256,128]{1,0:T(8,128)S(1)} %broadcast_in_dim.26.refs_0_, s32[8,512]{1,0:T(8,128)S(1)} %add_add_fusion.refs_1_, bf16[2048,256]{1,0:T(8,128)(2,1)S(1)} %pack_queries.1.refs_2_, ...), custom_call_target="tpu_custom_call", output_to_operand_aliasing={{0}: (6, {}), {1}: (7, {}), {2}: (8, {})} | custom-call | flops 4294967296 | bytes 1048576 | tf_op jit(solution)/shard_map/pallas_call | solution.py:207
  74.3 4.7 %shard_map.77 = bf16[256,1024]{1,0:T(8,128)(2,1)} custom-call(s32[256,128]{1,0:T(8,128)S(1)} %broadcast_in_dim.26.refs_0_, s32[8,512]{1,0:T(8,128)S(1)} %add_add_fusion.refs_1_, bf16[2048,256]{1,0:T(8,128)(2,1)S(1)} %pack_queries.1.refs_2_, bf16[1024,512]{1,0:T(8,128)(2,1)S(1)} %bitcast.15, bf16[32,16,576]{2,1,0:T(8,128)(2,1)S(1)} %collective-permute-done.2.refs_4_, ...), custom_call_target="tpu_custom_call" | custom-call | flops 2147483648 | bytes 1048576 | tf_op jit(solution)/shard_map/pallas_call | solution.py:207
  (24 shorter events, 0.7 us)
Async XLA Ops:
  0.0 48.3 %copy-start = (bf16[8,128,512]{2,1,0:T(8,128)(2,1)S(1)}, bf16[8,128,512]{2,1,0:T(8,128)(2,1)}, u32[]{:S(2)}) copy-start(bf16[8,128,512]{2,1,0:T(8,128)(2,1)} %param.11) | copy-start | bytes 3145732
  1.7 30.5 %all-to-all-start = ((bf16[32,16,576]{2,1,0:T(8,128)(2,1)}), bf16[32,16,576]{2,1,0:T(8,128)(2,1)S(1)}, u32[]{:S(2)}, u32[]{:S(2)}) async-start(bf16[32,16,576]{2,1,0:T(8,128)(2,1)} %broadcast_in_dim.46), calls=%async_computation | async-start | bytes 1310720 | tf_op jit(solution)/shard_map/all_to_all | solution.py:227
  32.3 9.2 %collective-permute-start.3 = (bf16[32,16,576]{2,1,0:T(8,128)(2,1)S(1)}, bf16[32,16,576]{2,1,0:T(8,128)(2,1)S(1)}, u32[]{:S(2)}, u32[]{:S(2)}) collective-permute-start(bf16[32,16,576]{2,1,0:T(8,128)(2,1)S(1)} %all-to-all-done.refs_4_), channel_id=1, source_target_pairs={{0,1},{1,0},{2,3},{3,2},{4,5},{5,4},{6,7},{7,6},{8,9},{9,8},{10,11... | collective-permute-start | bytes 1769480 | tf_op jit(solution)/shard_map/ppermute | solution.py:37
  34.8 10.3 %collective-permute-start = (bf16[32,16,576]{2,1,0:T(8,128)(2,1)S(1)}, bf16[32,16,576]{2,1,0:T(8,128)(2,1)S(1)}, u32[]{:S(2)}, u32[]{:S(2)}) collective-permute-start(bf16[32,16,576]{2,1,0:T(8,128)(2,1)S(1)} %all-to-all-done.refs_4_), channel_id=1, source_target_pairs={{0,8},{1,137},{8,128},{9,1},{128,136},{129,9},{136,0},{137,129},{2... | collective-permute-start | bytes 1769480 | tf_op jit(solution)/shard_map/ppermute | solution.py:33
  38.5 1.0 %copy-start.2 = (bf16[256,1024]{1,0:T(8,128)(2,1)S(1)}, bf16[256,1024]{1,0:T(8,128)(2,1)}, u32[]{:S(2)}) copy-start(bf16[256,1024]{1,0:T(8,128)(2,1)} %qn.1) | copy-start | bytes 1572868
  39.5 0.9 %copy-start.3 = (bf16[256,512]{1,0:T(8,128)(2,1)S(1)}, bf16[256,512]{1,0:T(8,128)(2,1)}, u32[]{:S(2)}) copy-start(bf16[256,512]{1,0:T(8,128)(2,1)} %qr.1) | copy-start | bytes 786436
  41.5 14.1 %collective-permute-start.4 = (bf16[32,16,576]{2,1,0:T(8,128)(2,1)S(1)}, bf16[32,16,576]{2,1,0:T(8,128)(2,1)S(1)}, u32[]{:S(2)}, u32[]{:S(2)}) collective-permute-start(bf16[32,16,576]{2,1,0:T(8,128)(2,1)S(1)} %collective-permute-done.3.refs_5_), channel_id=1, source_target_pairs={{0,8},{1,137},{8,128},{9,1},{128,136},{129,9},{136,0},{137,129},{2... | collective-permute-start | bytes 1769480 | tf_op jit(solution)/shard_map/ppermute | solution.py:33
  45.1 15.6 %collective-permute-start.6 = (bf16[32,16,576]{2,1,0:T(8,128)(2,1)S(1)}, bf16[32,16,576]{2,1,0:T(8,128)(2,1)S(1)}, u32[]{:S(2)}, u32[]{:S(2)}) collective-permute-start(bf16[32,16,576]{2,1,0:T(8,128)(2,1)S(1)} %collective-permute-done.refs_4_), channel_id=1, source_target_pairs={{0,1},{1,0},{2,3},{3,2},{4,5},{5,4},{6,7},{7,6},{8,9},{9,8},{10,11... | collective-permute-start | bytes 1769480 | tf_op jit(solution)/shard_map/ppermute | solution.py:37
  46.7 12.5 %collective-permute-start.1 = (bf16[32,16,576]{2,1,0:T(8,128)(2,1)S(1)}, bf16[32,16,576]{2,1,0:T(8,128)(2,1)S(1)}, u32[]{:S(2)}, u32[]{:S(2)}) collective-permute-start(bf16[32,16,576]{2,1,0:T(8,128)(2,1)S(1)} %collective-permute-done.refs_4_), channel_id=1, source_target_pairs={{0,8},{1,137},{8,128},{9,1},{128,136},{129,9},{136,0},{137,129},{2... | collective-permute-start | bytes 1769480 | tf_op jit(solution)/shard_map/ppermute | solution.py:33
  55.6 11.9 %collective-permute-start.5 = (bf16[32,16,576]{2,1,0:T(8,128)(2,1)S(1)}, bf16[32,16,576]{2,1,0:T(8,128)(2,1)S(1)}, u32[]{:S(2)}, u32[]{:S(2)}) collective-permute-start(bf16[32,16,576]{2,1,0:T(8,128)(2,1)S(1)} %collective-permute-done.4.refs_5_), channel_id=1, source_target_pairs={{0,1},{1,0},{2,3},{3,2},{4,5},{5,4},{6,7},{7,6},{8,9},{9,8},{10,11... | collective-permute-start | bytes 1769480 | tf_op jit(solution)/shard_map/ppermute | solution.py:37
  59.2 15.2 %collective-permute-start.2 = (bf16[32,16,576]{2,1,0:T(8,128)(2,1)S(1)}, bf16[32,16,576]{2,1,0:T(8,128)(2,1)S(1)}, u32[]{:S(2)}, u32[]{:S(2)}) collective-permute-start(bf16[32,16,576]{2,1,0:T(8,128)(2,1)S(1)} %collective-permute-done.1.refs_5_), channel_id=1, source_target_pairs={{0,1},{1,0},{2,3},{3,2},{4,5},{5,4},{6,7},{7,6},{8,9},{9,8},{10,11... | collective-permute-start | bytes 1769480 | tf_op jit(solution)/shard_map/ppermute | solution.py:37
  67.5 6.8 %copy-start.1 = (bf16[8,512,128]{2,1,0:T(8,128)(2,1)S(1)}, bf16[8,512,128]{2,1,0:T(8,128)(2,1)}, u32[]{:S(2)}) copy-start(bf16[8,512,128]{2,1,0:T(8,128)(2,1)} %refs_5_.1) | copy-start | bytes 3145732
where the time goes:
time: 79.4 us; the launch traced here: 79.1 us
  Pallas kernels  29 us (37%)
  starting transfers between devices  22.3 us (28%)
  waiting for transfers between devices  20.9 us (26%)
  local copies, waits for them, and re-layouts  5.68 us (7%)
  other arithmetic  0.98 us (1%)
    pallas_call x5, Pallas kernels, attend_call(): pl.pallas_call(functools.partial(attend, first, last, ids), out_shape=out...  28.8 us
    all_to_all x1, waiting for transfers between devices, compute(): plane = lax.all_to_all(copies, ('z', 'x'), 0, 0, tiled=True)  17.7 us
    all_to_all x1, starting transfers between devices, compute(): plane = lax.all_to_all(copies, ('z', 'x'), 0, 0, tiled=True)  11.9 us
    ppermute x4, starting transfers between devices, exchange(): return lax.ppermute(value, 'c', [(0, 1), (1, 0)])  5.65 us
    ppermute x3, starting transfers between devices, ring_step(): return lax.ppermute(value, ('yh', 'yl', 'c'), pairs)  4.81 us
    ppermute x3, waiting for transfers between devices, ring_step(): return lax.ppermute(value, ('yh', 'yl', 'c'), pairs)  3.25 us
    unnamed x8, local copies, waits for them, and re-layouts  2 us
    broadcast_in_dim x1, local copies, waits for them, and re-layouts, compute(): copies = jnp.broadcast_to(kv_latent[None], (32, *kv_latent.shape))  1.71 us
  transfers between devices with their start and end apart: 8, of which 3 were waited for; matrix products, arithmetic and copies ran while one was open for 4% of the time, Pallas kernels for 31%

commit v1 on v0

v1 whole, which is shorter than its diff:
```python
import functools

import jax
import jax.numpy as jnp
from jax import lax
from jax.experimental import pallas as pl
from jax.experimental.pallas import tpu as pltpu
from jax.sharding import Mesh
from jax.sharding import PartitionSpec as P


HEADS = 8
ROWS = 256
NOPE = 128
LATENT = 512
ROPE = 64
PIECE = 512
SCALE = (NOPE + ROPE) ** -0.5 * 1.4426950408889634
LOW = -1e30
NT = (((1,), (1,)), ((), ()))
NN = (((1,), (0,)), ((), ()))
HEAD_TILE = 4
TILES = HEADS // HEAD_TILE
NY = 4
CALLS = ((0,), (1,), (2,), (3, 4), (5, 6), (7,))


def ring_step(value):
    pairs = [
        (y * 2 + c, ((y + (1 - 2 * c)) % NY) * 2 + c) for y in range(NY) for c in range(2)
    ]
    return lax.ppermute(value, ("yh", "yl", "c"), pairs)


def exchange(value):
    return lax.ppermute(value, "c", [(0, 1), (1, 0)])


def prepare(half_order, qn, qr, weight, qx, wuk, qpos, kpos):
    zeros = jnp.zeros((ROWS, 64), jnp.bfloat16)
    wuk[...] = weight[...]
    for h in range(HEADS):
        rows = slice(h * ROWS, (h + 1) * ROWS)
        qx[rows, 0:128] = qn[:, h * 128 : (h + 1) * 128]
        qx[rows, 128:256] = jnp.concatenate([qr[:, h * 64 : (h + 1) * 64], zeros], axis=1)
    y = lax.axis_index("yh") * 2 + lax.axis_index("yl")
    z, c = lax.axis_index("z"), lax.axis_index("c")
    row = lax.broadcasted_iota(jnp.int32, (128, 128), 0)
    for n in range(2):
        block = half_order[(lax.axis_index("yh") * 8 + z) * 2 + n]
        qpos[n * 128 : (n + 1) * 128, :] = row + block * 128
    lane = lax.broadcasted_iota(jnp.int32, (8, PIECE), 1)
    inner = ((lane >> 4) & 3) * 32 + (lane & 15)
    ahead = 1 - 2 * c
    origins = (
        (y, c),
        (y, 1 - c),
        (y - ahead, c),
        (y + ahead, 1 - c),
        (y - ahead, 1 - c),
        (y + ahead, c),
        (y + 2, c),
        (y + 2, 1 - c),
    )
    for n, (ys, cs) in enumerate(origins):
        ys = ys & 3
        pos = inner + cs * 16
        for k in range(8):
            block = half_order[((ys >> 1) * 8 + k) * 2 + (ys & 1)]
            pos = jnp.where(lane >> 6 == k, pos + block * 128, pos)
        kpos[n : n + 1, :] = pos[0:1]


def attend(first, last, ids, *refs):
    f32, bf16 = jnp.float32, jnp.bfloat16
    refs = list(refs)
    take = lambda n: [refs.pop(0) for _ in range(n)]
    qpos, kpos, qx, wuk = take(4)
    pieces = take(len(ids))
    wuv = take(1)[0] if last else None
    state = None if first else take(3)
    if last:
        out = take(1)[0]
        acc, mref, lref = state
    else:
        acc, mref, lref = take(3)
    kn, kr, sbuf = take(3)
    zk = jnp.zeros((PIECE, 64), bf16)

    def latents():
        parts = [p[:, :, 0:LATENT].reshape(PIECE, LATENT) for p in pieces]
        return parts[0] if len(parts) == 1 else jnp.concatenate(parts, axis=0)

    def expand(tile):
        a, b = tile * HEAD_TILE * 128, (tile + 1) * HEAD_TILE * 128
        for n, p in enumerate(pieces):
            kn[n * PIECE : (n + 1) * PIECE, a:b] = lax.dot_general(
                p[:, :, 0:LATENT].reshape(PIECE, LATENT),
                wuk[a:b, :],
                NT,
                preferred_element_type=f32,
            ).astype(bf16)

    def score(tile, i):
        h = tile * HEAD_TILE + i
        keys = jnp.concatenate([kn[:, h * 128 : (h + 1) * 128], kr[...]], axis=1)
        sbuf[tile % 2, i * ROWS : (i + 1) * ROWS, :] = lax.dot_general(
            qx[h * ROWS : (h + 1) * ROWS, :], keys, NT, preferred_element_type=f32
        )

    def weigh(tile, i):
        r0 = (tile * HEAD_TILE + i) * ROWS
        r1 = r0 + ROWS
        a, b = i * ROWS, (i + 1) * ROWS
        qp = qpos[...]
        s = []
        for n, piece in enumerate(ids):
            for c in range(0, PIECE, 128):
                keep = kpos[piece : piece + 1, c : c + 128] <= qp
                at = n * PIECE + c
                s.append(jnp.where(keep, sbuf[tile % 2, a:b, at : at + 128], LOW))
        top = jnp.max(functools.reduce(jnp.maximum, s), axis=1, keepdims=True)
        if first:
            new = jnp.broadcast_to(top, (ROWS, 128))
        else:
            old = mref[r0:r1, :]
            new = jnp.maximum(old, top)
            factor = jnp.exp2((old - new) * SCALE)
        base = new * SCALE
        w = [jnp.exp2(v * SCALE - base) for v in s]
        total = functools.reduce(jnp.add, w)
        if not first:
            total = lref[r0:r1, :] * factor + total
        wb = jnp.concatenate([v.astype(bf16) for v in w], axis=1)
        product = lax.dot_general(wb, latents(), NN, preferred_element_type=f32)
        if first:
            acc[r0:r1, :] = product
        else:
            product = [
                acc[r0:r1, c : c + 128] * factor + product[:, c : c + 128]
                for c in range(0, LATENT, 128)
            ]
        mref[r0:r1, :] = new
        lref[r0:r1, :] = total
        if not first:
            for n, v in enumerate(product):
                acc[r0:r1, n * 128 : (n + 1) * 128] = v

    def finish(h):
        r0 = h * ROWS
        share = 1.0 / jnp.sum(lref[r0 : r0 + ROWS, :], axis=1, keepdims=True)
        latent = (acc[r0 : r0 + ROWS, :] * share).astype(bf16)
        out[:, h * 128 : (h + 1) * 128] = jnp.dot(
            latent, wuv[h], preferred_element_type=f32
        ).astype(bf16)

    for n, p in enumerate(pieces):
        kr[n * PIECE : (n + 1) * PIECE, :] = jnp.concatenate(
            [p[:, :, LATENT:].reshape(PIECE, ROPE), zk], axis=1
        )
    expand(0)
    for i in range(HEAD_TILE):
        score(0, i)
    for tile in range(TILES):
        if tile + 1 < TILES:
            expand(tile + 1)
        for i in range(HEAD_TILE):
            if tile + 1 < TILES:
                score(tile + 1, i)
            weigh(tile, i)
    if last:
        for h in range(HEADS):
            finish(h)


def attend_call(first, last, ids, qpos, kpos, qx, wuk, pieces, wuv, state):
    vmem = pltpu.VMEM
    f32, bf16 = jnp.float32, jnp.bfloat16
    args = [qpos, kpos, qx, wuk, *pieces]
    if last:
        args.append(wuv)
    alias = {}
    if not first:
        if not last:
            alias = {len(args) + i: i for i in range(3)}
        args.extend(state)
    shapes = [
        jax.ShapeDtypeStruct((HEADS * ROWS, LATENT), f32),
        jax.ShapeDtypeStruct((HEADS * ROWS, 128), f32),
        jax.ShapeDtypeStruct((HEADS * ROWS, 128), f32),
    ]
    keys = len(ids) * PIECE
    scratch = [
        vmem((keys, HEADS * 128), bf16),
        vmem((keys, 128), bf16),
        vmem((2, HEAD_TILE * ROWS, keys), f32),
    ]
    out_shape = jax.ShapeDtypeStruct((ROWS, HEADS * 128), bf16) if last else shapes
    spec = pl.BlockSpec(memory_space=vmem)
    return pl.pallas_call(
        functools.partial(attend, first, last, ids),
        out_shape=out_shape,
        in_specs=[spec] * len(args),
        out_specs=spec if last else [spec] * 3,
        scratch_shapes=scratch,
        input_output_aliases=alias,
        compiler_params=pltpu.CompilerParams(vmem_limit_bytes=14 << 20),
        cost_estimate=pl.CostEstimate(
            flops=2 * HEADS * ROWS * keys * 1024,
            bytes_accessed=1 << 20,
            transcendentals=HEADS * ROWS * keys,
        ),
    )(*args)


def compute(q_nope, q_rope, kv_latent, half_order, w_uk, w_uv):
    copies = jnp.broadcast_to(kv_latent[None], (32, *kv_latent.shape))
    plane = lax.all_to_all(copies, ("z", "x"), 0, 0, tiled=True)
    spec = pl.BlockSpec(memory_space=pltpu.VMEM)
    qx, wuk, qpos, kpos = pl.pallas_call(
        prepare,
        out_shape=[
            jax.ShapeDtypeStruct((HEADS * ROWS, 256), jnp.bfloat16),
            jax.ShapeDtypeStruct((HEADS * NOPE, LATENT), jnp.bfloat16),
            jax.ShapeDtypeStruct((ROWS, 128), jnp.int32),
            jax.ShapeDtypeStruct((8, PIECE), jnp.int32),
        ],
        in_specs=[pl.BlockSpec(memory_space=pltpu.SMEM), spec, spec, spec],
        out_specs=[spec] * 4,
        compiler_params=pltpu.CompilerParams(vmem_limit_bytes=8 << 20),
        name="prepare",
    )(half_order, q_nope, q_rope, w_uk.reshape(HEADS * NOPE, LATENT))
    first = ring_step(plane)
    other = exchange(plane)
    second = ring_step(other)
    third = ring_step(first)
    first_other = exchange(first)
    second_other = exchange(second)
    third_other = exchange(third)
    pieces = (plane, other, first, first_other, second, second_other, third, third_other)
    state = None
    for n, ids in enumerate(CALLS):
        state = attend_call(
            n == 0,
            n == len(CALLS) - 1,
            ids,
            qpos,
            kpos,
            qx,
            wuk,
            [pieces[i] for i in ids],
            w_uv,
            state,
        )
    return state


def solution(mesh):
    split = Mesh(mesh.devices.reshape(2, 8, 2, 4, 2), ("yh", "z", "yl", "x", "c"))
    ctx, head = ("yh", "z"), ("yl", "x", "c")
    return jax.shard_map(
        compute,
        mesh=split,
        in_specs=(
            P(ctx, head),
            P(ctx, head),
            P((*ctx, *head), None),
            P(),
            P(head, None, None),
            P(head, None, None),
        ),
        out_specs=P(ctx, head),
        check_vma=False,
    )
```

time: 79.4 us -> 76 us (0.957)
  blocking collectives: 0 us -> 30.3 us
  waiting for transfers between devices: 20.9 us -> 2.36 us
  starting transfers between devices: 22.3 us -> 11.9 us
  Pallas kernels: 29 us -> 26.4 us
  local copies, waits for them, and re-layouts: 5.68 us -> 4.65 us
  other arithmetic: 0.98 us -> 0 us
    all_to_all x0 -> x1, blocking collectives: none -> 30.3 us  [compute(): plane = lax.all_to_all(copies, ('z', 'x'), 0, 0, tiled=True)]
    all_to_all x1 -> x0, waiting for transfers between devices: 17.7 us -> none  [compute(): plane = lax.all_to_all(copies, ('z', 'x'), 0, 0, tiled=True)]
    all_to_all x1 -> x0, starting transfers between devices: 11.9 us -> none  [compute(): plane = lax.all_to_all(copies, ('z', 'x'), 0, 0, tiled=True)]
    pallas_call x5 -> x6, Pallas kernels: 28.8 us -> 25.4 us  [attend_call(): pl.pallas_call(functools.partial(attend, first, last, ids), out_shape=out...]
    unnamed x8 -> x10, local copies, waits for them, and re-layouts: 2 us -> 3.88 us
    ppermute x3, starting transfers between devices: 4.81 us -> 6.04 us  [ring_step(): return lax.ppermute(value, ('yh', 'yl', 'c'), pairs)]
    broadcast_in_dim x1, local copies, waits for them, and re-layouts: 1.71 us -> 0.78 us  [compute(): copies = jnp.broadcast_to(kv_latent[None], (32, *kv_latent.shape))]
    ppermute x3, waiting for transfers between devices: 3.25 us -> 2.35 us  [ring_step(): return lax.ppermute(value, ('yh', 'yl', 'c'), pairs)]
  transfers between devices with their start and end apart: 8 -> 7, of which waited for: 3 -> 2; matrix products, arithmetic and copies ran while one was open for 4% -> 0% of each run, Pallas kernels for 31% -> 28%
where the time goes in v1:
time: 76 us; the launch traced here: 75.7 us
  blocking collectives  30.3 us (40%)
  Pallas kernels  26.4 us (35%)
  starting transfers between devices  11.9 us (16%)
  local copies, waits for them, and re-layouts  4.65 us (6%)
  waiting for transfers between devices  2.36 us (3%)
    all_to_all x1, blocking collectives, compute(): plane = lax.all_to_all(copies, ('z', 'x'), 0, 0, tiled=True)  30.3 us
    pallas_call x6, Pallas kernels, attend_call(): pl.pallas_call(functools.partial(attend, first, last, ids), out_shape=out...  25.4 us
    ppermute x3, starting transfers between devices, ring_step(): return lax.ppermute(value, ('yh', 'yl', 'c'), pairs)  6.04 us
    ppermute x4, starting transfers between devices, exchange(): return lax.ppermute(value, 'c', [(0, 1), (1, 0)])  5.83 us
    unnamed x10, local copies, waits for them, and re-layouts  3.88 us
    ppermute x3, waiting for transfers between devices, ring_step(): return lax.ppermute(value, ('yh', 'yl', 'c'), pairs)  2.35 us
  transfers between devices with their start and end apart: 7, of which 2 were waited for; matrix products, arithmetic and copies ran while one was open for 0% of the time, Pallas kernels for 28%

profile of v1, /device:TPU:1, one launch (start us, length us, event | category | flops | bytes accessed | tf_op | source)
XLA Modules:
  0.0 75.7 jit_solution(12486627185087292353)
XLA Ops:
  0.0 0.8 %broadcast_in_dim.2 = bf16[32,16,576]{2,1,0:T(8,128)(2,1)S(1)} broadcast(bf16[16,576]{1,0:T(8,128)(2,1)} %param.8), dimensions={1,2} | broadcast | bytes 608256 | tf_op jit(solution)/shard_map/broadcast_in_dim | solution.py:217
  0.8 30.3 %all_to_all.5.refs_4_ = bf16[32,16,576]{2,1,0:T(8,128)(2,1)S(1)} all-to-all(bf16[32,16,576]{2,1,0:T(8,128)(2,1)S(1)} %broadcast_in_dim.2), channel_id=1, replica_groups=mesh['yh'=2,'z'=8,'yl'=2,'x'=4,'c'=2] {'z','x'}, dimensions={0} | all-to-all | bytes 1179648 | tf_op jit(solution)/shard_map/all_to_all | solution.py:218
  31.1 2.5 %collective-permute-start.3 = (bf16[32,16,576]{2,1,0:T(8,128)(2,1)S(1)}, bf16[32,16,576]{2,1,0:T(8,128)(2,1)S(1)}, u32[]{:S(2)}, u32[]{:S(2)}) collective-permute-start(bf16[32,16,576]{2,1,0:T(8,128)(2,1)S(1)} %all_to_all.5.refs_4_), channel_id=1, source_target_pairs={{0,1},{1,0},{2,3},{3,2},{4,5},{5,4},{6,7},{7,6},{8,9},{9,8},{10,11... | collective-permute-start | bytes 1769480 | tf_op jit(solution)/shard_map/ppermute | solution.py:36
  33.6 2.7 %collective-permute-start = (bf16[32,16,576]{2,1,0:T(8,128)(2,1)S(1)}, bf16[32,16,576]{2,1,0:T(8,128)(2,1)S(1)}, u32[]{:S(2)}, u32[]{:S(2)}) collective-permute-start(bf16[32,16,576]{2,1,0:T(8,128)(2,1)S(1)} %all_to_all.5.refs_4_), channel_id=1, source_target_pairs={{0,8},{1,137},{8,128},{9,1},{128,136},{129,9},{136,0},{137,129},{2... | collective-permute-start | bytes 1769480 | tf_op jit(solution)/shard_map/ppermute | solution.py:32
  36.3 1.7 %collective-permute-start.4 = (bf16[32,16,576]{2,1,0:T(8,128)(2,1)S(1)}, bf16[32,16,576]{2,1,0:T(8,128)(2,1)S(1)}, u32[]{:S(2)}, u32[]{:S(2)}) collective-permute-start(bf16[32,16,576]{2,1,0:T(8,128)(2,1)S(1)} %collective-permute-done.3.refs_4_), channel_id=1, source_target_pairs={{0,8},{1,137},{8,128},{9,1},{128,136},{129,9},{136,0},{137,129},{2... | collective-permute-start | bytes 1769480 | tf_op jit(solution)/shard_map/ppermute | solution.py:32
  38.1 1.2 %copy-done = bf16[8,128,512]{2,1,0:T(8,128)(2,1)S(1)} copy-done((bf16[8,128,512]{2,1,0:T(8,128)(2,1)S(1)}, bf16[8,128,512]{2,1,0:T(8,128)(2,1)}, u32[]{:S(2)}) %copy-start) | copy-done | bytes 1048600
  39.3 1.0 %copy-done.2 = bf16[256,1024]{1,0:T(8,128)(2,1)S(1)} copy-done((bf16[256,1024]{1,0:T(8,128)(2,1)S(1)}, bf16[256,1024]{1,0:T(8,128)(2,1)}, u32[]{:S(2)}) %copy-start.2) | copy-done | bytes 524312
  40.3 0.9 %copy-done.3 = bf16[256,512]{1,0:T(8,128)(2,1)S(1)} copy-done((bf16[256,512]{1,0:T(8,128)(2,1)S(1)}, bf16[256,512]{1,0:T(8,128)(2,1)}, u32[]{:S(2)}) %copy-start.3) | copy-done | bytes 262168
  41.3 0.7 copy-done.4
  41.9 0.9 %prepare.1 = (bf16[2048,256]{1,0:T(8,128)(2,1)S(1)}, bf16[1024,512]{1,0:T(8,128)(2,1)S(1)}, s32[256,128]{1,0:T(8,128)S(1)}, s32[8,512]{1,0:T(8,128)S(1)}) custom-call(s32[32]{0:T(128)S(1)} %copy-done.4, bf16[256,1024]{1,0:T(8,128)(2,1)S(1)} %copy-done.2, bf16[256,512]{1,0:T(8,128)(2,1)S(1)} %copy-done.3, bf16[1024,512]{1,0:T(8,128)(2,1)S(1)} %bitcast.1), custom_call_target="tpu_custom_call" | custom-call | tf_op jit(solution)/shard_map/prepare/pallas_call | solution.py:220
  42.9 1.0 %collective-permute-done.refs_4_ = bf16[32,16,576]{2,1,0:T(8,128)(2,1)S(1)} collective-permute-done((bf16[32,16,576]{2,1,0:T(8,128)(2,1)S(1)}, bf16[32,16,576]{2,1,0:T(8,128)(2,1)S(1)}, u32[]{:S(2)}, u32[]{:S(2)}) %collective-permute-start) | collective-permute-done | bytes 589856 | tf_op jit(solution)/shard_map/ppermute | solution.py:32
  43.9 1.5 %collective-permute-start.6 = (bf16[32,16,576]{2,1,0:T(8,128)(2,1)S(1)}, bf16[32,16,576]{2,1,0:T(8,128)(2,1)S(1)}, u32[]{:S(2)}, u32[]{:S(2)}) collective-permute-start(bf16[32,16,576]{2,1,0:T(8,128)(2,1)S(1)} %collective-permute-done.refs_4_), channel_id=1, source_target_pairs={{0,1},{1,0},{2,3},{3,2},{4,5},{5,4},{6,7},{7,6},{8,9},{9,8},{10,11... | collective-permute-start | bytes 1769480 | tf_op jit(solution)/shard_map/ppermute | solution.py:36
  45.4 1.6 %collective-permute-start.1 = (bf16[32,16,576]{2,1,0:T(8,128)(2,1)S(1)}, bf16[32,16,576]{2,1,0:T(8,128)(2,1)S(1)}, u32[]{:S(2)}, u32[]{:S(2)}) collective-permute-start(bf16[32,16,576]{2,1,0:T(8,128)(2,1)S(1)} %collective-permute-done.refs_4_), channel_id=1, source_target_pairs={{0,8},{1,137},{8,128},{9,1},{128,136},{129,9},{136,0},{137,129},{2... | collective-permute-start | bytes 1769480 | tf_op jit(solution)/shard_map/ppermute | solution.py:32
  47.0 2.9 %shard_map.64 = (f32[2048,512]{1,0:T(8,128)S(1)}, f32[2048,128]{1,0:T(8,128)S(1)}, f32[2048,128]{1,0:T(8,128)S(1)}) custom-call(s32[256,128]{1,0:T(8,128)S(1)} %get-tuple-element.24.refs_0_, s32[8,512]{1,0:T(8,128)S(1)} %get-tuple-element.25.refs_1_, bf16[2048,256]{1,0:T(8,128)(2,1)S(1)} %get-tuple-element.26.refs_2_, ...), custom_call_target="tpu_custom_call" | custom-call | flops 2147483648 | bytes 1048576 | tf_op jit(solution)/shard_map/pallas_call | solution.py:200
  49.9 3.2 %shard_map.65 = (f32[2048,512]{1,0:T(8,128)S(1)}, f32[2048,128]{1,0:T(8,128)S(1)}, f32[2048,128]{1,0:T(8,128)S(1)}) custom-call(s32[256,128]{1,0:T(8,128)S(1)} %get-tuple-element.24.refs_0_, s32[8,512]{1,0:T(8,128)S(1)} %get-tuple-element.25.refs_1_, ...), custom_call_target="tpu_custom_call", output_to_operand_aliasing={{0}: (5, {}), {1}: (6, {}), {2}: (7, {})} | custom-call | flops 2147483648 | bytes 1048576 | tf_op jit(solution)/shard_map/pallas_call | solution.py:200
  53.1 0.3 collective-permute-start.5
  53.4 3.2 %shard_map.66 = (f32[2048,512]{1,0:T(8,128)S(1)}, f32[2048,128]{1,0:T(8,128)S(1)}, f32[2048,128]{1,0:T(8,128)S(1)}) custom-call(s32[256,128]{1,0:T(8,128)S(1)} %get-tuple-element.24.refs_0_, s32[8,512]{1,0:T(8,128)S(1)} %get-tuple-element.25.refs_1_, ...), custom_call_target="tpu_custom_call", output_to_operand_aliasing={{0}: (5, {}), {1}: (6, {}), {2}: (7, {})} | custom-call | flops 2147483648 | bytes 1048576 | tf_op jit(solution)/shard_map/pallas_call | solution.py:200
  56.6 1.3 %collective-permute-done.1.refs_5_ = bf16[32,16,576]{2,1,0:T(8,128)(2,1)S(1)} collective-permute-done((bf16[32,16,576]{2,1,0:T(8,128)(2,1)S(1)}, bf16[32,16,576]{2,1,0:T(8,128)(2,1)S(1)}, u32[]{:S(2)}, u32[]{:S(2)}) %collective-permute-start.1) | collective-permute-done | bytes 589856 | tf_op jit(solution)/shard_map/ppermute | solution.py:32
  57.9 1.5 %collective-permute-start.2 = (bf16[32,16,576]{2,1,0:T(8,128)(2,1)S(1)}, bf16[32,16,576]{2,1,0:T(8,128)(2,1)S(1)}, u32[]{:S(2)}, u32[]{:S(2)}) collective-permute-start(bf16[32,16,576]{2,1,0:T(8,128)(2,1)S(1)} %collective-permute-done.1.refs_5_), channel_id=1, source_target_pairs={{0,1},{1,0},{2,3},{3,2},{4,5},{5,4},{6,7},{7,6},{8,9},{9,8},{10,11... | collective-permute-start | bytes 1769480 | tf_op jit(solution)/shard_map/ppermute | solution.py:36
  59.5 5.6 %shard_map.67 = (f32[2048,512]{1,0:T(8,128)S(1)}, f32[2048,128]{1,0:T(8,128)S(1)}, f32[2048,128]{1,0:T(8,128)S(1)}) custom-call(s32[256,128]{1,0:T(8,128)S(1)} %get-tuple-element.24.refs_0_, s32[8,512]{1,0:T(8,128)S(1)} %get-tuple-element.25.refs_1_, ...), custom_call_target="tpu_custom_call", output_to_operand_aliasing={{0}: (6, {}), {1}: (7, {}), {2}: (8, {})} | custom-call | flops 4294967296 | bytes 1048576 | tf_op jit(solution)/shard_map/pallas_call | solution.py:200
  65.1 0.0 collective-permute-done.5.refs_4_
  65.1 0.0 copy-start.1
  65.1 5.6 %shard_map.68 = (f32[2048,512]{1,0:T(8,128)S(1)}, f32[2048,128]{1,0:T(8,128)S(1)}, f32[2048,128]{1,0:T(8,128)S(1)}) custom-call(s32[256,128]{1,0:T(8,128)S(1)} %get-tuple-element.24.refs_0_, s32[8,512]{1,0:T(8,128)S(1)} %get-tuple-element.25.refs_1_, ...), custom_call_target="tpu_custom_call", output_to_operand_aliasing={{0}: (6, {}), {1}: (7, {}), {2}: (8, {})} | custom-call | flops 4294967296 | bytes 1048576 | tf_op jit(solution)/shard_map/pallas_call | solution.py:200
  70.8 4.9 %shard_map.69 = bf16[256,1024]{1,0:T(8,128)(2,1)} custom-call(s32[256,128]{1,0:T(8,128)S(1)} %get-tuple-element.24.refs_0_, s32[8,512]{1,0:T(8,128)S(1)} %get-tuple-element.25.refs_1_, bf16[2048,256]{1,0:T(8,128)(2,1)S(1)} %get-tuple-element.26.refs_2_, bf16[1024,512]{1,0:T(8,128)(2,1)S(1)} %get-tuple-element.27.refs_3_, ...), custom_call_target="tpu_custom_call" | custom-call | flops 2147483648 | bytes 1048576 | tf_op jit(solution)/shard_map/pallas_call | solution.py:200
  (9 shorter events, 0.0 us)
Async XLA Ops:
  31.1 5.2 %collective-permute-start.3 = (bf16[32,16,576]{2,1,0:T(8,128)(2,1)S(1)}, bf16[32,16,576]{2,1,0:T(8,128)(2,1)S(1)}, u32[]{:S(2)}, u32[]{:S(2)}) collective-permute-start(bf16[32,16,576]{2,1,0:T(8,128)(2,1)S(1)} %all_to_all.5.refs_4_), channel_id=1, source_target_pairs={{0,1},{1,0},{2,3},{3,2},{4,5},{5,4},{6,7},{7,6},{8,9},{9,8},{10,11... | collective-permute-start | bytes 1769480 | tf_op jit(solution)/shard_map/ppermute | solution.py:36
  33.6 10.3 %collective-permute-start = (bf16[32,16,576]{2,1,0:T(8,128)(2,1)S(1)}, bf16[32,16,576]{2,1,0:T(8,128)(2,1)S(1)}, u32[]{:S(2)}, u32[]{:S(2)}) collective-permute-start(bf16[32,16,576]{2,1,0:T(8,128)(2,1)S(1)} %all_to_all.5.refs_4_), channel_id=1, source_target_pairs={{0,8},{1,137},{8,128},{9,1},{128,136},{129,9},{136,0},{137,129},{2... | collective-permute-start | bytes 1769480 | tf_op jit(solution)/shard_map/ppermute | solution.py:32
  36.3 16.8 %collective-permute-start.4 = (bf16[32,16,576]{2,1,0:T(8,128)(2,1)S(1)}, bf16[32,16,576]{2,1,0:T(8,128)(2,1)S(1)}, u32[]{:S(2)}, u32[]{:S(2)}) collective-permute-start(bf16[32,16,576]{2,1,0:T(8,128)(2,1)S(1)} %collective-permute-done.3.refs_4_), channel_id=1, source_target_pairs={{0,8},{1,137},{8,128},{9,1},{128,136},{129,9},{136,0},{137,129},{2... | collective-permute-start | bytes 1769480 | tf_op jit(solution)/shard_map/ppermute | solution.py:32
  38.1 1.2 %copy-start = (bf16[8,128,512]{2,1,0:T(8,128)(2,1)S(1)}, bf16[8,128,512]{2,1,0:T(8,128)(2,1)}, u32[]{:S(2)}) copy-start(bf16[8,128,512]{2,1,0:T(8,128)(2,1)} %param.10) | copy-start | bytes 3145732
  39.3 1.0 %copy-start.2 = (bf16[256,1024]{1,0:T(8,128)(2,1)S(1)}, bf16[256,1024]{1,0:T(8,128)(2,1)}, u32[]{:S(2)}) copy-start(bf16[256,1024]{1,0:T(8,128)(2,1)} %qn.1) | copy-start | bytes 1572868
  40.3 0.9 %copy-start.3 = (bf16[256,512]{1,0:T(8,128)(2,1)S(1)}, bf16[256,512]{1,0:T(8,128)(2,1)}, u32[]{:S(2)}) copy-start(bf16[256,512]{1,0:T(8,128)(2,1)} %qr.1) | copy-start | bytes 786436
  41.3 0.7 copy-start.4
  43.9 15.6 %collective-permute-start.6 = (bf16[32,16,576]{2,1,0:T(8,128)(2,1)S(1)}, bf16[32,16,576]{2,1,0:T(8,128)(2,1)S(1)}, u32[]{:S(2)}, u32[]{:S(2)}) collective-permute-start(bf16[32,16,576]{2,1,0:T(8,128)(2,1)S(1)} %collective-permute-done.refs_4_), channel_id=1, source_target_pairs={{0,1},{1,0},{2,3},{3,2},{4,5},{5,4},{6,7},{7,6},{8,9},{9,8},{10,11... | collective-permute-start | bytes 1769480 | tf_op jit(solution)/shard_map/ppermute | solution.py:36
  45.4 12.5 %collective-permute-start.1 = (bf16[32,16,576]{2,1,0:T(8,128)(2,1)S(1)}, bf16[32,16,576]{2,1,0:T(8,128)(2,1)S(1)}, u32[]{:S(2)}, u32[]{:S(2)}) collective-permute-start(bf16[32,16,576]{2,1,0:T(8,128)(2,1)S(1)} %collective-permute-done.refs_4_), channel_id=1, source_target_pairs={{0,8},{1,137},{8,128},{9,1},{128,136},{129,9},{136,0},{137,129},{2... | collective-permute-start | bytes 1769480 | tf_op jit(solution)/shard_map/ppermute | solution.py:32
  53.1 12.0 %collective-permute-start.5 = (bf16[32,16,576]{2,1,0:T(8,128)(2,1)S(1)}, bf16[32,16,576]{2,1,0:T(8,128)(2,1)S(1)}, u32[]{:S(2)}, u32[]{:S(2)}) collective-permute-start(bf16[32,16,576]{2,1,0:T(8,128)(2,1)S(1)} %collective-permute-done.4.refs_5_), channel_id=1, source_target_pairs={{0,1},{1,0},{2,3},{3,2},{4,5},{5,4},{6,7},{7,6},{8,9},{9,8},{10,11... | collective-permute-start | bytes 1769480 | tf_op jit(solution)/shard_map/ppermute | solution.py:36
  57.9 12.9 %collective-permute-start.2 = (bf16[32,16,576]{2,1,0:T(8,128)(2,1)S(1)}, bf16[32,16,576]{2,1,0:T(8,128)(2,1)S(1)}, u32[]{:S(2)}, u32[]{:S(2)}) collective-permute-start(bf16[32,16,576]{2,1,0:T(8,128)(2,1)S(1)} %collective-permute-done.1.refs_5_), channel_id=1, source_target_pairs={{0,1},{1,0},{2,3},{3,2},{4,5},{5,4},{6,7},{7,6},{8,9},{9,8},{10,11... | collective-permute-start | bytes 1769480 | tf_op jit(solution)/shard_map/ppermute | solution.py:36
  65.1 5.7 %copy-start.1 = (bf16[8,512,128]{2,1,0:T(8,128)(2,1)S(1)}, bf16[8,512,128]{2,1,0:T(8,128)(2,1)}, u32[]{:S(2)}) copy-start(bf16[8,512,128]{2,1,0:T(8,128)(2,1)} %refs_5_.1) | copy-start | bytes 3145732

commit v2 on v1

--- a/solution.py
+++ b/solution.py
@@ -22,7 +22,7 @@
 HEAD_TILE = 4
 TILES = HEADS // HEAD_TILE
 NY = 4
-CALLS = ((0,), (1,), (2,), (3, 4), (5, 6), (7,))
+CALLS = ((0,), (1,), (2,), (3,), (4,), (5,), (6,), (7,))
 
 
 def ring_step(value):
@@ -36,13 +36,21 @@
     return lax.ppermute(value, "c", [(0, 1), (1, 0)])
 
 
-def prepare(half_order, qn, qr, weight, qx, wuk, qpos, kpos):
-    zeros = jnp.zeros((ROWS, 64), jnp.bfloat16)
-    wuk[...] = weight[...]
-    for h in range(HEADS):
-        rows = slice(h * ROWS, (h + 1) * ROWS)
-        qx[rows, 0:128] = qn[:, h * 128 : (h + 1) * 128]
-        qx[rows, 128:256] = jnp.concatenate([qr[:, h * 64 : (h + 1) * 64], zeros], axis=1)
+def spread(kv, copies):
+    x = kv[...]
+    parts = [x[0:8, 0:LATENT], x[8:16, 0:LATENT], x[0:8, LATENT:], x[8:16, LATENT:]]
+    row = jnp.concatenate(parts, axis=1)
+    for n in range(32):
+        copies[n] = row
+
+
+def prepare(half_order, qn_hbm, qr_hbm, weight, qx, wuk, qpos, kpos, qn, qr, sems):
+    moves = [
+        pltpu.make_async_copy(source, target, sems.at[n])
+        for n, (source, target) in enumerate(((qn_hbm, qn), (qr_hbm, qr), (weight, wuk)))
+    ]
+    for move in moves:
+        move.start()
     y = lax.axis_index("yh") * 2 + lax.axis_index("yl")
     z, c = lax.axis_index("z"), lax.axis_index("c")
     row = lax.broadcasted_iota(jnp.int32, (128, 128), 0)
@@ -50,7 +58,8 @@
         block = half_order[(lax.axis_index("yh") * 8 + z) * 2 + n]
         qpos[n * 128 : (n + 1) * 128, :] = row + block * 128
     lane = lax.broadcasted_iota(jnp.int32, (8, PIECE), 1)
-    inner = ((lane >> 4) & 3) * 32 + (lane & 15)
+    inner = ((lane >> 3) & 3) * 32 + (lane & 7) + (lane >> 8) * 8
+    peer_z = (lane >> 5) & 7
     ahead = 1 - 2 * c
     origins = (
         (y, c),
@@ -67,8 +76,15 @@
         pos = inner + cs * 16
         for k in range(8):
             block = half_order[((ys >> 1) * 8 + k) * 2 + (ys & 1)]
-            pos = jnp.where(lane >> 6 == k, pos + block * 128, pos)
+            pos = jnp.where(peer_z == k, pos + block * 128, pos)
         kpos[n : n + 1, :] = pos[0:1]
+    for move in moves:
+        move.wait()
+    zeros = jnp.zeros((ROWS, 64), jnp.bfloat16)
+    for h in range(HEADS):
+        rows = slice(h * ROWS, (h + 1) * ROWS)
+        qx[rows, 0:128] = qn[:, h * 128 : (h + 1) * 128]
+        qx[rows, 128:256] = jnp.concatenate([qr[:, h * 64 : (h + 1) * 64], zeros], axis=1)
 
 
 def attend(first, last, ids, *refs):
@@ -85,17 +101,16 @@
     else:
         acc, mref, lref = take(3)
     kn, kr, sbuf = take(3)
-    zk = jnp.zeros((PIECE, 64), bf16)
-
-    def latents():
-        parts = [p[:, :, 0:LATENT].reshape(PIECE, LATENT) for p in pieces]
-        return parts[0] if len(parts) == 1 else jnp.concatenate(parts, axis=0)
+    zk = jnp.zeros((PIECE // 2, 64), bf16)
+
+    def latents(which):
+        return jnp.concatenate([p[:, a : a + LATENT] for p in which for a in (0, LATENT)], axis=0)
 
     def expand(tile):
         a, b = tile * HEAD_TILE * 128, (tile + 1) * HEAD_TILE * 128
         for n, p in enumerate(pieces):
             kn[n * PIECE : (n + 1) * PIECE, a:b] = lax.dot_general(
-                p[:, :, 0:LATENT].reshape(PIECE, LATENT),
+                latents([p]),
                 wuk[a:b, :],
                 NT,
                 preferred_element_type=f32,
@@ -132,7 +147,7 @@
         if not first:
             total = lref[r0:r1, :] * factor + total
         wb = jnp.concatenate([v.astype(bf16) for v in w], axis=1)
-        product = lax.dot_general(wb, latents(), NN, preferred_element_type=f32)
+        product = lax.dot_general(wb, latents(pieces), NN, preferred_element_type=f32)
         if first:
             acc[r0:r1, :] = product
         else:
@@ -155,9 +170,9 @@
         ).astype(bf16)
 
     for n, p in enumerate(pieces):
-        kr[n * PIECE : (n + 1) * PIECE, :] = jnp.concatenate(
-            [p[:, :, LATENT:].reshape(PIECE, ROPE), zk], axis=1
-        )
+        for k in range(2):
+            r0, c0 = n * PIECE + k * PIECE // 2, 2 * LATENT + k * ROPE
+            kr[r0 : r0 + PIECE // 2, :] = jnp.concatenate([p[:, c0 : c0 + ROPE], zk], axis=1)
     expand(0)
     for i in range(HEAD_TILE):
         score(0, i)
@@ -168,9 +183,11 @@
             if tile + 1 < TILES:
                 score(tile + 1, i)
             weigh(tile, i)
+            if last and tile:
+                finish((tile - 1) * HEAD_TILE + i)
     if last:
-        for h in range(HEADS):
-            finish(h)
+        for i in range(HEAD_TILE):
+            finish((TILES - 1) * HEAD_TILE + i)
 
 
 def attend_call(first, last, ids, qpos, kpos, qx, wuk, pieces, wuv, state):
@@ -214,9 +231,18 @@
 
 
 def compute(q_nope, q_rope, kv_latent, half_order, w_uk, w_uv):
-    copies = jnp.broadcast_to(kv_latent[None], (32, *kv_latent.shape))
+    spec = pl.BlockSpec(memory_space=pltpu.VMEM)
+    width = 2 * (LATENT + ROPE)
+    copies = pl.pallas_call(
+        spread,
+        out_shape=jax.ShapeDtypeStruct((32, 8, width), jnp.bfloat16),
+        in_specs=[spec],
+        out_specs=spec,
+        compiler_params=pltpu.CompilerParams(vmem_limit_bytes=4 << 20),
+        name="spread",
+    )(kv_latent)
     plane = lax.all_to_all(copies, ("z", "x"), 0, 0, tiled=True)
-    spec = pl.BlockSpec(memory_space=pltpu.VMEM)
+    plane = plane.reshape(PIECE // 2, width)
     qx, wuk, qpos, kpos = pl.pallas_call(
         prepare,
         out_shape=[
@@ -225,8 +251,14 @@
             jax.ShapeDtypeStruct((ROWS, 128), jnp.int32),
             jax.ShapeDtypeStruct((8, PIECE), jnp.int32),
         ],
-        in_specs=[pl.BlockSpec(memory_space=pltpu.SMEM), spec, spec, spec],
+        in_specs=[pl.BlockSpec(memory_space=pltpu.SMEM)]
+        + [pl.BlockSpec(memory_space=pltpu.HBM)] * 3,
         out_specs=[spec] * 4,
+        scratch_shapes=[
+            pltpu.VMEM((ROWS, HEADS * NOPE), jnp.bfloat16),
+            pltpu.VMEM((ROWS, HEADS * ROPE), jnp.bfloat16),
+            pltpu.SemaphoreType.DMA((3,)),
+        ],
         compiler_params=pltpu.CompilerParams(vmem_limit_bytes=8 << 20),
         name="prepare",
     )(half_order, q_nope, q_rope, w_uk.reshape(HEADS * NOPE, LATENT))

time: 76 us -> 73.9 us (0.972)
  waiting for transfers between devices: 2.36 us -> 0.27 us
  Pallas kernels: 26.4 us -> 27.8 us
  blocking collectives: 30.3 us -> 29.2 us
    ppermute x3, waiting for transfers between devices: 2.35 us -> 0.26 us  [ring_step(): return lax.ppermute(value, ('yh', 'yl', 'c'), pairs)]
    pallas_call x6 -> x8, Pallas kernels: 25.4 us -> 26.6 us  [attend_call(): pl.pallas_call(functools.partial(attend, first, last, ids), out_shape=out...]
    all_to_all x1, blocking collectives: 30.3 us -> 29.2 us  [compute(): plane = lax.all_to_all(copies, ('z', 'x'), 0, 0, tiled=True)]
    broadcast_in_dim x1 -> x0, local copies, waits for them, and re-layouts: 0.78 us -> none  [compute(): copies = jnp.broadcast_to(kv_latent[None], (32, *kv_latent.shape))]
    unnamed x10 -> x12, local copies, waits for them, and re-layouts: 3.88 us -> 4.6 us
  transfers between devices with their start and end apart: 7 -> 7, of which waited for: 2 -> 1; matrix products, arithmetic and copies ran while one was open for 0% -> 0% of each run, Pallas kernels for 28% -> 31%
where the time goes in v2:
time: 73.9 us; the launch traced here: 73.6 us
  blocking collectives  29.2 us (40%)
  Pallas kernels  27.8 us (38%)
  starting transfers between devices  11.7 us (16%)
  local copies, waits for them, and re-layouts  4.6 us (6%)
    all_to_all x1, blocking collectives, compute(): plane = lax.all_to_all(copies, ('z', 'x'), 0, 0, tiled=True)  29.2 us
    pallas_call x8, Pallas kernels, attend_call(): pl.pallas_call(functools.partial(attend, first, last, ids), out_shape=out...  26.6 us
    ppermute x3, starting transfers between devices, ring_step(): return lax.ppermute(value, ('yh', 'yl', 'c'), pairs)  5.95 us
    ppermute x4, starting transfers between devices, exchange(): return lax.ppermute(value, 'c', [(0, 1), (1, 0)])  5.72 us
    unnamed x12, local copies, waits for them, and re-layouts  4.6 us
  transfers between devices with their start and end apart: 7, of which 1 were waited for; matrix products, arithmetic and copies ran while one was open for 0% of the time, Pallas kernels for 31%

profile of v2, /device:TPU:1, one launch (start us, length us, event | category | flops | bytes accessed | tf_op | source)
XLA Modules:
  0.0 73.6 jit_solution(17629019497235418970)
XLA Ops:
  0.0 0.7 copy-done.4
  0.7 0.1 spread.1
  0.8 29.2 %all_to_all.5 = bf16[32,8,1152]{2,1,0:T(8,128)(2,1)S(1)} all-to-all(bf16[32,8,1152]{2,1,0:T(8,128)(2,1)S(1)} %spread.1), channel_id=1, replica_groups=mesh['yh'=2,'z'=8,'yl'=2,'x'=4,'c'=2] {'z','x'}, dimensions={0} | all-to-all | bytes 1179648 | tf_op jit(solution)/shard_map/all_to_all | solution.py:244
  30.0 2.4 %collective-permute-start.3 = (bf16[256,1152]{1,0:T(8,128)(2,1)S(1)}, bf16[256,1152]{1,0:T(8,128)(2,1)S(1)}, u32[]{:S(2)}, u32[]{:S(2)}) collective-permute-start(bf16[256,1152]{1,0:T(8,128)(2,1)S(1)} %bitcast.3), channel_id=1, source_target_pairs={{0,1},{1,0},{2,3},{3,2},{4,5},{5,4},{6,7},{7,6},{8,9},{9,8},{10,11... | collective-permute-start | bytes 1769480 | tf_op jit(solution)/shard_map/ppermute | solution.py:36
  32.4 2.7 %collective-permute-start = (bf16[256,1152]{1,0:T(8,128)(2,1)S(1)}, bf16[256,1152]{1,0:T(8,128)(2,1)S(1)}, u32[]{:S(2)}, u32[]{:S(2)}) collective-permute-start(bf16[256,1152]{1,0:T(8,128)(2,1)S(1)} %bitcast.4), channel_id=1, source_target_pairs={{0,8},{1,137},{8,128},{9,1},{128,136},{129,9},{136,0},{137,129},{2... | collective-permute-start | bytes 1769480 | tf_op jit(solution)/shard_map/ppermute | solution.py:32
  35.2 1.6 %collective-permute-start.4 = (bf16[256,1152]{1,0:T(8,128)(2,1)S(1)}, bf16[256,1152]{1,0:T(8,128)(2,1)S(1)}, u32[]{:S(2)}, u32[]{:S(2)}) collective-permute-start(bf16[256,1152]{1,0:T(8,128)(2,1)S(1)} %collective-permute-done.3.refs_4_), channel_id=1, source_target_pairs={{0,8},{1,137},{8,128},{9,1},{128,136},{129,9},{136,0},{137,129},{2... | collective-permute-start | bytes 1769480 | tf_op jit(solution)/shard_map/ppermute | solution.py:32
  36.8 1.2 %copy-done = bf16[8,128,512]{2,1,0:T(8,128)(2,1)S(1)} copy-done((bf16[8,128,512]{2,1,0:T(8,128)(2,1)S(1)}, bf16[8,128,512]{2,1,0:T(8,128)(2,1)}, u32[]{:S(2)}) %copy-start) | copy-done | bytes 1048600
  38.0 1.0 %copy-done.2 = bf16[256,1024]{1,0:T(8,128)(2,1)S(1)} copy-done((bf16[256,1024]{1,0:T(8,128)(2,1)S(1)}, bf16[256,1024]{1,0:T(8,128)(2,1)}, u32[]{:S(2)}) %copy-start.2) | copy-done | bytes 524312
  39.0 0.9 %copy-done.3 = bf16[256,512]{1,0:T(8,128)(2,1)S(1)} copy-done((bf16[256,512]{1,0:T(8,128)(2,1)S(1)}, bf16[256,512]{1,0:T(8,128)(2,1)}, u32[]{:S(2)}) %copy-start.3) | copy-done | bytes 262168
  40.0 0.7 copy-done.5
  40.7 1.1 %prepare.1 = (bf16[2048,256]{1,0:T(8,128)(2,1)S(1)}, bf16[1024,512]{1,0:T(8,128)(2,1)S(1)}, s32[256,128]{1,0:T(8,128)S(1)}, s32[8,512]{1,0:T(8,128)S(1)}) custom-call(s32[32]{0:T(128)S(1)} %copy-done.5, bf16[256,1024]{1,0:T(8,128)(2,1)S(1)} %copy-done.2, bf16[256,512]{1,0:T(8,128)(2,1)S(1)} %copy-done.3, bf16[1024,512]{1,0:T(8,128)(2,1)S(1)} %bitcast.2), custom_call_target="tpu_custom_call" | custom-call | tf_op jit(solution)/shard_map/prepare/pallas_call | solution.py:246
  41.8 0.2 collective-permute-done.refs_4_
  42.0 1.5 %collective-permute-start.6 = (bf16[256,1152]{1,0:T(8,128)(2,1)S(1)}, bf16[256,1152]{1,0:T(8,128)(2,1)S(1)}, u32[]{:S(2)}, u32[]{:S(2)}) collective-permute-start(bf16[256,1152]{1,0:T(8,128)(2,1)S(1)} %collective-permute-done.refs_4_), channel_id=1, source_target_pairs={{0,1},{1,0},{2,3},{3,2},{4,5},{5,4},{6,7},{7,6},{8,9},{9,8},{10,11... | collective-permute-start | bytes 1769480 | tf_op jit(solution)/shard_map/ppermute | solution.py:36
  43.5 1.6 %collective-permute-start.1 = (bf16[256,1152]{1,0:T(8,128)(2,1)S(1)}, bf16[256,1152]{1,0:T(8,128)(2,1)S(1)}, u32[]{:S(2)}, u32[]{:S(2)}) collective-permute-start(bf16[256,1152]{1,0:T(8,128)(2,1)S(1)} %collective-permute-done.refs_4_), channel_id=1, source_target_pairs={{0,8},{1,137},{8,128},{9,1},{128,136},{129,9},{136,0},{137,129},{2... | collective-permute-start | bytes 1769480 | tf_op jit(solution)/shard_map/ppermute | solution.py:32
  45.1 2.9 %shard_map.64 = (f32[2048,512]{1,0:T(8,128)S(1)}, f32[2048,128]{1,0:T(8,128)S(1)}, f32[2048,128]{1,0:T(8,128)S(1)}) custom-call(s32[256,128]{1,0:T(8,128)S(1)} %get-tuple-element.30.refs_0_, s32[8,512]{1,0:T(8,128)S(1)} %get-tuple-element.31.refs_1_, bf16[2048,256]{1,0:T(8,128)(2,1)S(1)} %get-tuple-element.32.refs_2_, ...), custom_call_target="tpu_custom_call" | custom-call | flops 2147483648 | bytes 1048576 | tf_op jit(solution)/shard_map/pallas_call | solution.py:217
  48.0 3.1 %shard_map.65 = (f32[2048,512]{1,0:T(8,128)S(1)}, f32[2048,128]{1,0:T(8,128)S(1)}, f32[2048,128]{1,0:T(8,128)S(1)}) custom-call(s32[256,128]{1,0:T(8,128)S(1)} %get-tuple-element.30.refs_0_, s32[8,512]{1,0:T(8,128)S(1)} %get-tuple-element.31.refs_1_, ...), custom_call_target="tpu_custom_call", output_to_operand_aliasing={{0}: (5, {}), {1}: (6, {}), {2}: (7, {})} | custom-call | flops 2147483648 | bytes 1048576 | tf_op jit(solution)/shard_map/pallas_call | solution.py:217
  51.2 0.3 collective-permute-start.5
  51.4 3.1 %shard_map.66 = (f32[2048,512]{1,0:T(8,128)S(1)}, f32[2048,128]{1,0:T(8,128)S(1)}, f32[2048,128]{1,0:T(8,128)S(1)}) custom-call(s32[256,128]{1,0:T(8,128)S(1)} %get-tuple-element.30.refs_0_, s32[8,512]{1,0:T(8,128)S(1)} %get-tuple-element.31.refs_1_, ...), custom_call_target="tpu_custom_call", output_to_operand_aliasing={{0}: (5, {}), {1}: (6, {}), {2}: (7, {})} | custom-call | flops 2147483648 | bytes 1048576 | tf_op jit(solution)/shard_map/pallas_call | solution.py:217
  54.6 1.5 %collective-permute-start.2 = (bf16[256,1152]{1,0:T(8,128)(2,1)S(1)}, bf16[256,1152]{1,0:T(8,128)(2,1)S(1)}, u32[]{:S(2)}, u32[]{:S(2)}) collective-permute-start(bf16[256,1152]{1,0:T(8,128)(2,1)S(1)} %collective-permute-done.1.refs_4_), channel_id=1, source_target_pairs={{0,1},{1,0},{2,3},{3,2},{4,5},{5,4},{6,7},{7,6},{8,9},{9,8},{10,11... | collective-permute-start | bytes 1769480 | tf_op jit(solution)/shard_map/ppermute | solution.py:36
  56.2 3.1 %shard_map.67 = (f32[2048,512]{1,0:T(8,128)S(1)}, f32[2048,128]{1,0:T(8,128)S(1)}, f32[2048,128]{1,0:T(8,128)S(1)}) custom-call(s32[256,128]{1,0:T(8,128)S(1)} %get-tuple-element.30.refs_0_, s32[8,512]{1,0:T(8,128)S(1)} %get-tuple-element.31.refs_1_, ...), custom_call_target="tpu_custom_call", output_to_operand_aliasing={{0}: (5, {}), {1}: (6, {}), {2}: (7, {})} | custom-call | flops 2147483648 | bytes 1048576 | tf_op jit(solution)/shard_map/pallas_call | solution.py:217
  59.3 3.1 %shard_map.68 = (f32[2048,512]{1,0:T(8,128)S(1)}, f32[2048,128]{1,0:T(8,128)S(1)}, f32[2048,128]{1,0:T(8,128)S(1)}) custom-call(s32[256,128]{1,0:T(8,128)S(1)} %get-tuple-element.30.refs_0_, s32[8,512]{1,0:T(8,128)S(1)} %get-tuple-element.31.refs_1_, ...), custom_call_target="tpu_custom_call", output_to_operand_aliasing={{0}: (5, {}), {1}: (6, {}), {2}: (7, {})} | custom-call | flops 2147483648 | bytes 1048576 | tf_op jit(solution)/shard_map/pallas_call | solution.py:217
  62.5 3.1 %shard_map.69 = (f32[2048,512]{1,0:T(8,128)S(1)}, f32[2048,128]{1,0:T(8,128)S(1)}, f32[2048,128]{1,0:T(8,128)S(1)}) custom-call(s32[256,128]{1,0:T(8,128)S(1)} %get-tuple-element.30.refs_0_, s32[8,512]{1,0:T(8,128)S(1)} %get-tuple-element.31.refs_1_, ...), custom_call_target="tpu_custom_call", output_to_operand_aliasing={{0}: (5, {}), {1}: (6, {}), {2}: (7, {})} | custom-call | flops 2147483648 | bytes 1048576 | tf_op jit(solution)/shard_map/pallas_call | solution.py:217
  65.6 3.1 %shard_map.70 = (f32[2048,512]{1,0:T(8,128)S(1)}, f32[2048,128]{1,0:T(8,128)S(1)}, f32[2048,128]{1,0:T(8,128)S(1)}) custom-call(s32[256,128]{1,0:T(8,128)S(1)} %get-tuple-element.30.refs_0_, s32[8,512]{1,0:T(8,128)S(1)} %get-tuple-element.31.refs_1_, ...), custom_call_target="tpu_custom_call", output_to_operand_aliasing={{0}: (5, {}), {1}: (6, {}), {2}: (7, {})} | custom-call | flops 2147483648 | bytes 1048576 | tf_op jit(solution)/shard_map/pallas_call | solution.py:217
  68.8 4.9 %shard_map.71 = bf16[256,1024]{1,0:T(8,128)(2,1)} custom-call(s32[256,128]{1,0:T(8,128)S(1)} %get-tuple-element.30.refs_0_, s32[8,512]{1,0:T(8,128)S(1)} %get-tuple-element.31.refs_1_, bf16[2048,256]{1,0:T(8,128)(2,1)S(1)} %get-tuple-element.32.refs_2_, bf16[1024,512]{1,0:T(8,128)(2,1)S(1)} %get-tuple-element.33.refs_3_, ...), custom_call_target="tpu_custom_call" | custom-call | flops 2147483648 | bytes 1048576 | tf_op jit(solution)/shard_map/pallas_call | solution.py:217
  (13 shorter events, 0.1 us)
Async XLA Ops:
  0.0 0.7 copy-start.4
  30.0 5.1 %collective-permute-start.3 = (bf16[256,1152]{1,0:T(8,128)(2,1)S(1)}, bf16[256,1152]{1,0:T(8,128)(2,1)S(1)}, u32[]{:S(2)}, u32[]{:S(2)}) collective-permute-start(bf16[256,1152]{1,0:T(8,128)(2,1)S(1)} %bitcast.3), channel_id=1, source_target_pairs={{0,1},{1,0},{2,3},{3,2},{4,5},{5,4},{6,7},{7,6},{8,9},{9,8},{10,11... | collective-permute-start | bytes 1769480 | tf_op jit(solution)/shard_map/ppermute | solution.py:36
  32.4 9.6 %collective-permute-start = (bf16[256,1152]{1,0:T(8,128)(2,1)S(1)}, bf16[256,1152]{1,0:T(8,128)(2,1)S(1)}, u32[]{:S(2)}, u32[]{:S(2)}) collective-permute-start(bf16[256,1152]{1,0:T(8,128)(2,1)S(1)} %bitcast.4), channel_id=1, source_target_pairs={{0,8},{1,137},{8,128},{9,1},{128,136},{129,9},{136,0},{137,129},{2... | collective-permute-start | bytes 1769480 | tf_op jit(solution)/shard_map/ppermute | solution.py:32
  35.2 16.0 %collective-permute-start.4 = (bf16[256,1152]{1,0:T(8,128)(2,1)S(1)}, bf16[256,1152]{1,0:T(8,128)(2,1)S(1)}, u32[]{:S(2)}, u32[]{:S(2)}) collective-permute-start(bf16[256,1152]{1,0:T(8,128)(2,1)S(1)} %collective-permute-done.3.refs_4_), channel_id=1, source_target_pairs={{0,8},{1,137},{8,128},{9,1},{128,136},{129,9},{136,0},{137,129},{2... | collective-permute-start | bytes 1769480 | tf_op jit(solution)/shard_map/ppermute | solution.py:32
  36.8 1.2 %copy-start = (bf16[8,128,512]{2,1,0:T(8,128)(2,1)S(1)}, bf16[8,128,512]{2,1,0:T(8,128)(2,1)}, u32[]{:S(2)}) copy-start(bf16[8,128,512]{2,1,0:T(8,128)(2,1)} %param.10) | copy-start | bytes 3145732
  38.0 1.0 %copy-start.2 = (bf16[256,1024]{1,0:T(8,128)(2,1)S(1)}, bf16[256,1024]{1,0:T(8,128)(2,1)}, u32[]{:S(2)}) copy-start(bf16[256,1024]{1,0:T(8,128)(2,1)} %qn_hbm.1) | copy-start | bytes 1572868
  39.0 0.9 %copy-start.3 = (bf16[256,512]{1,0:T(8,128)(2,1)S(1)}, bf16[256,512]{1,0:T(8,128)(2,1)}, u32[]{:S(2)}) copy-start(bf16[256,512]{1,0:T(8,128)(2,1)} %qr_hbm.1) | copy-start | bytes 786436
  40.0 0.7 copy-start.5
  42.0 14.2 %collective-permute-start.6 = (bf16[256,1152]{1,0:T(8,128)(2,1)S(1)}, bf16[256,1152]{1,0:T(8,128)(2,1)S(1)}, u32[]{:S(2)}, u32[]{:S(2)}) collective-permute-start(bf16[256,1152]{1,0:T(8,128)(2,1)S(1)} %collective-permute-done.refs_4_), channel_id=1, source_target_pairs={{0,1},{1,0},{2,3},{3,2},{4,5},{5,4},{6,7},{7,6},{8,9},{9,8},{10,11... | collective-permute-start | bytes 1769480 | tf_op jit(solution)/shard_map/ppermute | solution.py:36
  43.5 11.1 %collective-permute-start.1 = (bf16[256,1152]{1,0:T(8,128)(2,1)S(1)}, bf16[256,1152]{1,0:T(8,128)(2,1)S(1)}, u32[]{:S(2)}, u32[]{:S(2)}) collective-permute-start(bf16[256,1152]{1,0:T(8,128)(2,1)S(1)} %collective-permute-done.refs_4_), channel_id=1, source_target_pairs={{0,8},{1,137},{8,128},{9,1},{128,136},{129,9},{136,0},{137,129},{2... | collective-permute-start | bytes 1769480 | tf_op jit(solution)/shard_map/ppermute | solution.py:32
  51.2 11.3 %collective-permute-start.5 = (bf16[256,1152]{1,0:T(8,128)(2,1)S(1)}, bf16[256,1152]{1,0:T(8,128)(2,1)S(1)}, u32[]{:S(2)}, u32[]{:S(2)}) collective-permute-start(bf16[256,1152]{1,0:T(8,128)(2,1)S(1)} %collective-permute-done.4.refs_4_), channel_id=1, source_target_pairs={{0,1},{1,0},{2,3},{3,2},{4,5},{5,4},{6,7},{7,6},{8,9},{9,8},{10,11... | collective-permute-start | bytes 1769480 | tf_op jit(solution)/shard_map/ppermute | solution.py:36
  54.6 14.1 %collective-permute-start.2 = (bf16[256,1152]{1,0:T(8,128)(2,1)S(1)}, bf16[256,1152]{1,0:T(8,128)(2,1)S(1)}, u32[]{:S(2)}, u32[]{:S(2)}) collective-permute-start(bf16[256,1152]{1,0:T(8,128)(2,1)S(1)} %collective-permute-done.1.refs_4_), channel_id=1, source_target_pairs={{0,1},{1,0},{2,3},{3,2},{4,5},{5,4},{6,7},{7,6},{8,9},{9,8},{10,11... | collective-permute-start | bytes 1769480 | tf_op jit(solution)/shard_map/ppermute | solution.py:36
  65.6 3.2 %copy-start.1 = (bf16[8,512,128]{2,1,0:T(8,128)(2,1)S(1)}, bf16[8,512,128]{2,1,0:T(8,128)(2,1)}, u32[]{:S(2)}) copy-start(bf16[8,512,128]{2,1,0:T(8,128)(2,1)} %refs_5_.1) | copy-start | bytes 3145732
